TPU v7x, 512 devices: a whole 4x4x16 slice. The times are simulated.
512 devices in a mesh: ctx: 32 (over y, x, z_hi), head: 16 (over z_lo, core).
Axes of the slice: x: 4, y: 4, z: 16 (z_hi: 2, z_lo: 8; z = z_hi * 8 + z_lo), core: 2. Of those that a mesh axis runs over, the one named last changes fastest.
Arguments:
- tokens: bfloat16 [14336, 5376], P('ctx'), may hold values from -6 to 6
- w_query: bfloat16 [5376, 4096], P('ctx', 'head')
- key_weight: bfloat16 [5376, 2048], P('ctx', 'head')
- value_weight: bfloat16 [5376, 2048], P('ctx', 'head'), may hold values from -0.078125 to 0.078125
- query_gain: float32 [128], replicated, may hold values from 0.5 to 16
- key_gain: float32 [128], replicated, may hold values from 0.5 to 16
Outputs:
- attended: bfloat16 [14336, 4096], P('ctx', 'head')
All inputs are finite; a program needn't handle non-finite values.
Results may differ from a plain program's by a relative error of at most 0.025.
Values may be sent and summed in bfloat16 or wider, within the bound.
No kernel may reach another device: no remote copies, remote signals or barrier semaphores. Data moves between devices by JAX's collectives and lax.ppermute only.
A program may use at most 64 MiB of HBM per device.

v0:
```python
import jax
import jax.numpy as jnp
from jax import lax
from jax.sharding import PartitionSpec as P

WINDOW = 1024
query_scale = 168.0 ** (-0.5)


def from_behind(block, axis, distance):
    devices = range(lax.axis_size(axis))
    route = [(i - distance, i) for i in devices if i - distance in devices]
    return lax.ppermute(block, axis, route)


def normalize(values, gain):
    return values * lax.rsqrt(jnp.mean(values * values, axis=-1, keepdims=True) + 1e-06) * gain


def rotate(values, position):
    half = values.shape[-1] // 2
    expo = jnp.arange(half, dtype=jnp.float32) * (2.0 / values.shape[-1])
    freq = jnp.power(jnp.float32(10000.0), -expo)
    angle = position[:, None] * freq[None, :]
    cosine = jnp.cos(angle)[:, None, :]
    sine = jnp.sin(angle)[:, None, :]
    first = values[..., :half]
    second = values[..., half:]
    return jnp.concatenate(
        [first * cosine - second * sine, second * cosine + first * sine], axis=-1
    )


def fold_rows(tokens, piece):
    return jnp.dot(tokens, piece, preferred_element_type=jnp.float32)


def on_device(tokens, w_query, key_weight, value_weight, query_gain, key_gain):
    row_count = tokens.shape[0]
    head_size = query_gain.shape[0]
    kv_local = key_weight.shape[1] // head_size
    q_width = w_query.shape[1]

    def add_one(piece):
        return fold_rows(tokens, piece)

    query_sum = add_one(lax.all_gather(w_query, "ctx", axis=0, tiled=True))
    summed_keys = add_one(lax.all_gather(key_weight, "ctx", axis=0, tiled=True))
    summed_values = add_one(lax.all_gather(value_weight, "ctx", axis=0, tiled=True))
    offset = lax.axis_index("ctx") * row_count
    local_pos = offset + jnp.arange(row_count, dtype=jnp.int32)
    position = local_pos.astype(jnp.float32)
    queries = rotate(
        normalize(query_sum.reshape(row_count, 2 * kv_local, head_size), query_gain), position
    ).astype(jnp.bfloat16)
    keys = rotate(
        normalize(summed_keys.reshape(row_count, kv_local, head_size), key_gain), position
    ).astype(jnp.bfloat16)
    values = summed_values.reshape(row_count, kv_local, head_size).astype(jnp.bfloat16)
    reach = WINDOW - 1
    hop_count = (reach + row_count - 1) // row_count
    needed = [min(row_count, reach - distance * row_count) for distance in range(hop_count)]
    received = []
    carried = (keys, values)
    for distance in range(hop_count):
        arrived = from_behind((carried[0], carried[1]), "ctx", 1)
        received.append(arrived)
        if distance + 1 < hop_count:
            keep = needed[distance + 1]
            cut = needed[distance] - keep
            carried = (arrived[0][cut:], arrived[1][cut:])
    all_keys = jnp.concatenate([piece[0] for piece in reversed(received)] + [keys], axis=0)
    all_values = jnp.concatenate([piece[1] for piece in reversed(received)] + [values], axis=0)
    key_pos = offset - reach + jnp.arange(reach + row_count, dtype=jnp.int32)
    allowed = (
        (key_pos[None, :] <= local_pos[:, None])
        & (key_pos[None, :] > local_pos[:, None] - WINDOW)
        & (key_pos[None, :] >= 0)
    )
    grouped_heads = queries.reshape(row_count, kv_local, 2, head_size)
    scores = (
        jnp.einsum("bkgd,ckd->kgbc", grouped_heads, all_keys, preferred_element_type=jnp.float32)
        * query_scale
    )
    scores = jnp.where(allowed[None, None], scores, jnp.float32(-1e30))
    top = jnp.max(scores, axis=-1, keepdims=True)
    weights = jnp.exp(scores - top)
    probs = (weights / jnp.sum(weights, axis=-1, keepdims=True)).astype(jnp.bfloat16)
    mixed = jnp.einsum("kgbc,ckd->bkgd", probs, all_values, preferred_element_type=jnp.float32)
    return mixed.reshape(row_count, q_width).astype(jnp.bfloat16)


def solution(mesh):
    placed = (P("ctx", None), P("ctx", "head"), P("ctx", "head"), P("ctx", "head"), P(), P())
    return jax.shard_map(
        on_device, mesh=mesh, in_specs=placed, out_specs=P("ctx", "head"), check_vma=False
    )
```

profile of v0, /device:TPU:2, one launch (start us, length us, event | category | flops | bytes accessed | tf_op | source)
XLA Modules:
  0.0 406.5 jit_solution(15615109111452498067)
XLA Ops:
  8.8 123.6 %all-gather.6.cloned.1.call-done = bf16[5376,128]{1,0:T(8,128)(2,1)} async-done(((bf16[168,128]{1,0:T(8,128)(2,1)}), bf16[5376,128]{1,0:T(8,128)(2,1)}) %all-gather.6.cloned.1.call-update) | async-done | bytes 1376272 | tf_op jit(solution)/shard_map/all_gather | solution.py:48
  132.3 4.3 %multiply_reduce_fusion.1 = (f32[448]{0:T(512)S(1)}, f32[448,128]{1,0:T(8,128)S(1)}) fusion(bf16[448,5376]{1,0:T(8,128)(2,1)} %param.6, bf16[5376,128]{1,0:T(8,128)(2,1)} %all-gather.6.cloned.1.call-done), kind=kOutput, calls=%fused_computation.35 | convolution fusion | flops 616676928 | bytes 6424320 | tf_op jit(solution)/shard_map/dot_general | solution.py:35
  136.8 1.1 fusion.18
  138.0 1.9 collective-permute-start.3
  139.9 104.3 %all-gather.4.cloned.1.call-done = bf16[5376,128]{1,0:T(8,128)(2,1)} async-done(((bf16[168,128]{1,0:T(8,128)(2,1)}), bf16[5376,128]{1,0:T(8,128)(2,1)}) %all-gather.4.cloned.1.call-update) | async-done | bytes 1376272 | tf_op jit(solution)/shard_map/all_gather | solution.py:49
  244.2 4.2 %fusion.9 = bf16[448,1,128]{2,0,1:T(8,128)(2,1)S(1)} fusion(bf16[448,5376]{1,0:T(8,128)(2,1)} %param.6, bf16[5376,128]{1,0:T(8,128)(2,1)} %all-gather.4.cloned.1.call-done), kind=kOutput, calls=%fused_computation.10 | convolution fusion | flops 616620032 | bytes 6307840 | tf_op jit(solution)/shard_map/dot_general | solution.py:35
  248.4 1.9 collective-permute-start
  250.4 13.2 %collective-permute-start.4 = (bf16[448,1,128]{2,0,1:T(8,128)(2,1)S(1)}, bf16[448,1,128]{2,0,1:T(8,128)(2,1)S(1)}, u32[]{:S(2)}, u32[]{:S(2)}) collective-permute-start(bf16[448,1,128]{2,0,1:T(8,128)(2,1)S(1)} %collective-permute-done.3), channel_id=1, source_target_pairs={{0,16},{16,32},{32,48},{48,64},{64,80},{80,96},{96,112},{112,128},... | collective-permute-start | bytes 344072 | tf_op jit(solution)/shard_map/ppermute | solution.py:13
  263.6 17.1 %collective-permute-done = bf16[448,1,128]{2,0,1:T(8,128)(2,1)S(1)} collective-permute-done((bf16[448,1,128]{2,0,1:T(8,128)(2,1)S(1)}, bf16[448,1,128]{2,0,1:T(8,128)(2,1)S(1)}, u32[]{:S(2)}, u32[]{:S(2)}) %collective-permute-start) | collective-permute-done | bytes 114720 | tf_op jit(solution)/shard_map/ppermute | solution.py:13
  280.7 1.9 collective-permute-start.1
  283.4 5.9 %collective-permute-done.4 = bf16[448,1,128]{2,0,1:T(8,128)(2,1)S(1)} collective-permute-done((bf16[448,1,128]{2,0,1:T(8,128)(2,1)S(1)}, bf16[448,1,128]{2,0,1:T(8,128)(2,1)S(1)}, u32[]{:S(2)}, u32[]{:S(2)}) %collective-permute-start.4) | collective-permute-done | bytes 114720 | tf_op jit(solution)/shard_map/ppermute | solution.py:13
  289.3 7.0 %collective-permute-start.5 = (bf16[127,1,128]{2,0,1:T(8,128)(2,1)S(1)}, bf16[127,1,128]{2,0,1:T(8,128)(2,1)S(1)}, u32[]{:S(2)}, u32[]{:S(2)}) collective-permute-start(bf16[127,1,128]{2,0,1:T(8,128)(2,1)S(1)} %slice.27), channel_id=1, source_target_pairs={{0,16},{16,32},{32,48},{48,64},{64,80},{80,96},{96,112},{112,128},... | collective-permute-start | bytes 97544 | tf_op jit(solution)/shard_map/ppermute | solution.py:13
  296.2 2.6 collective-permute-done.1
  298.8 5.2 %collective-permute-start.2 = (bf16[127,1,128]{2,0,1:T(8,128)(2,1)S(1)}, bf16[127,1,128]{2,0,1:T(8,128)(2,1)S(1)}, u32[]{:S(2)}, u32[]{:S(2)}) collective-permute-start(bf16[127,1,128]{2,0,1:T(8,128)(2,1)S(1)} %slice.24), channel_id=1, source_target_pairs={{0,16},{16,32},{32,48},{48,64},{64,80},{80,96},{96,112},{112,128},... | collective-permute-start | bytes 97544 | tf_op jit(solution)/shard_map/ppermute | solution.py:13
  304.0 0.9 multiply_cosine_fusion
  305.4 1.6 concatenate.26
  307.0 8.0 %collective-permute-done.2 = bf16[127,1,128]{2,0,1:T(8,128)(2,1)S(1)} collective-permute-done((bf16[127,1,128]{2,0,1:T(8,128)(2,1)S(1)}, bf16[127,1,128]{2,0,1:T(8,128)(2,1)S(1)}, u32[]{:S(2)}, u32[]{:S(2)}) %collective-permute-start.2) | collective-permute-done | bytes 32544 | tf_op jit(solution)/shard_map/ppermute | solution.py:13
  315.0 1.6 concatenate.24
  316.6 72.9 %all-gather.8.cloned.1.call-done = bf16[5376,256]{1,0:T(8,128)(2,1)} async-done(((bf16[168,256]{1,0:T(8,128)(2,1)}), bf16[5376,256]{1,0:T(8,128)(2,1)}) %all-gather.8.cloned.1.call-update) | async-done | bytes 2752528 | tf_op jit(solution)/shard_map/all_gather | solution.py:47
  389.5 4.6 %fusion.28 = f32[448,256]{1,0:T(8,128)S(1)} fusion(bf16[448,5376]{1,0:T(8,128)(2,1)} %param.6, bf16[5376,256]{1,0:T(8,128)(2,1)} %all-gather.8.cloned.1.call-done), kind=kOutput, calls=%fused_computation.47 | convolution fusion | flops 1233125376 | bytes 8028160 | tf_op jit(solution)/shard_map/dot_general | solution.py:35
  395.6 1.5 fusion.27
  397.1 0.9 fusion
  398.0 1.0 fusion.6
  399.2 0.7 copy.20
  (30 shorter events, 5.2 us)
Async XLA Ops:
  6.5 130.1 %copy-start.1 = (f32[128]{0:T(128)S(1)}, f32[128]{0:T(128)}, u32[]{:S(2)}) copy-start(f32[128]{0:T(128)} %param.11) | copy-start | bytes 1540
  6.5 125.8 %all-gather.6.cloned.1.call-start = ((), (), s32[]{:S(2)}) async-start(), calls=%async_computation.1 | async-start | bytes 1419264 | tf_op jit(solution)/shard_map/all_gather | solution.py:48
  7.3 236.9 %all-gather.4.cloned.1.call-start = ((), (), s32[]{:S(2)}) async-start(), calls=%async_computation | async-start | bytes 1419264 | tf_op jit(solution)/shard_map/all_gather | solution.py:49
  8.0 381.5 %all-gather.8.cloned.1.call-start = ((), (), s32[]{:S(2)}) async-start(), calls=%async_computation.2 | async-start | bytes 2838528 | tf_op jit(solution)/shard_map/all_gather | solution.py:47
  138.0 112.4 %collective-permute-start.3 = (bf16[448,1,128]{2,0,1:T(8,128)(2,1)S(1)}, bf16[448,1,128]{2,0,1:T(8,128)(2,1)S(1)}, u32[]{:S(2)}, u32[]{:S(2)}) collective-permute-start(bf16[448,1,128]{2,0,1:T(8,128)(2,1)S(1)} %pad_maximum_fusion), channel_id=1, source_target_pairs={{0,16},{16,32},{32,48},{48,64},{64,80},{80,96},{96,112},{112,128},... | collective-permute-start | bytes 344072 | tf_op jit(solution)/shard_map/ppermute | solution.py:13
  248.4 32.3 %collective-permute-start = (bf16[448,1,128]{2,0,1:T(8,128)(2,1)S(1)}, bf16[448,1,128]{2,0,1:T(8,128)(2,1)S(1)}, u32[]{:S(2)}, u32[]{:S(2)}) collective-permute-start(bf16[448,1,128]{2,0,1:T(8,128)(2,1)S(1)} %fusion.9), channel_id=1, source_target_pairs={{0,16},{16,32},{32,48},{48,64},{64,80},{80,96},{96,112},{112,128},... | collective-permute-start | bytes 344072 | tf_op jit(solution)/shard_map/ppermute | solution.py:13
  250.4 38.9 %collective-permute-start.4 = (bf16[448,1,128]{2,0,1:T(8,128)(2,1)S(1)}, bf16[448,1,128]{2,0,1:T(8,128)(2,1)S(1)}, u32[]{:S(2)}, u32[]{:S(2)}) collective-permute-start(bf16[448,1,128]{2,0,1:T(8,128)(2,1)S(1)} %collective-permute-done.3), channel_id=1, source_target_pairs={{0,16},{16,32},{32,48},{48,64},{64,80},{80,96},{96,112},{112,128},... | collective-permute-start | bytes 344072 | tf_op jit(solution)/shard_map/ppermute | solution.py:13
  280.7 18.0 %collective-permute-start.1 = (bf16[448,1,128]{2,0,1:T(8,128)(2,1)S(1)}, bf16[448,1,128]{2,0,1:T(8,128)(2,1)S(1)}, u32[]{:S(2)}, u32[]{:S(2)}) collective-permute-start(bf16[448,1,128]{2,0,1:T(8,128)(2,1)S(1)} %collective-permute-done), channel_id=1, source_target_pairs={{0,16},{16,32},{32,48},{48,64},{64,80},{80,96},{96,112},{112,128},... | collective-permute-start | bytes 344072 | tf_op jit(solution)/shard_map/ppermute | solution.py:13
  289.3 16.1 %collective-permute-start.5 = (bf16[127,1,128]{2,0,1:T(8,128)(2,1)S(1)}, bf16[127,1,128]{2,0,1:T(8,128)(2,1)S(1)}, u32[]{:S(2)}, u32[]{:S(2)}) collective-permute-start(bf16[127,1,128]{2,0,1:T(8,128)(2,1)S(1)} %slice.27), channel_id=1, source_target_pairs={{0,16},{16,32},{32,48},{48,64},{64,80},{80,96},{96,112},{112,128},... | collective-permute-start | bytes 97544 | tf_op jit(solution)/shard_map/ppermute | solution.py:13
  298.8 16.2 %collective-permute-start.2 = (bf16[127,1,128]{2,0,1:T(8,128)(2,1)S(1)}, bf16[127,1,128]{2,0,1:T(8,128)(2,1)S(1)}, u32[]{:S(2)}, u32[]{:S(2)}) collective-permute-start(bf16[127,1,128]{2,0,1:T(8,128)(2,1)S(1)} %slice.24), channel_id=1, source_target_pairs={{0,16},{16,32},{32,48},{48,64},{64,80},{80,96},{96,112},{112,128},... | collective-permute-start | bytes 97544 | tf_op jit(solution)/shard_map/ppermute | solution.py:13
  316.6 78.5 %copy-start = (f32[128]{0:T(128)S(1)}, f32[128]{0:T(128)}, u32[]{:S(2)}) copy-start(f32[128]{0:T(128)} %param.10) | copy-start | bytes 1540
Sparse Core Ops, SparseCore 0:
  11.7 120.5 all-gather.5
  136.7 107.4 all-gather.3
  248.6 140.9 all-gather.7
where the time goes:
time: 407 us; the launch traced here: 406 us
  waiting for transfers between devices  337 us (83%)
  starting transfers between devices  31.2 us (8%)
  matrix products  15.6 us (4%)
  between operations  13.3 us (3%)
  other arithmetic  4.81 us (1%)
  local copies, waits for them, and re-layouts  4.53 us (1%)
    all_gather x1, waiting for transfers between devices, on_device(): summed_keys = add_one(lax.all_gather(key_weight, 'ctx', axis=0, tiled=True))  124 us
    all_gather x1, waiting for transfers between devices, on_device(): lax.all_gather(value_weight, 'ctx', axis=0, tiled=True)  104 us
    all_gather x1, waiting for transfers between devices, on_device(): query_sum = add_one(lax.all_gather(w_query, 'ctx', axis=0, tiled=True))  72.9 us
    ppermute x6, waiting for transfers between devices, from_behind(): return lax.ppermute(block, axis, route)  34.1 us
    ppermute x6, starting transfers between devices, from_behind(): return lax.ppermute(block, axis, route)  31.2 us
    dot_general x3, matrix products, fold_rows(): return jnp.dot(tokens, piece, preferred_element_type=jnp.float32)  13.1 us
  transfers between devices with their start and end apart: 9, of which 8 were waited for; matrix products, arithmetic and copies ran while one was open for 4% of the time, Pallas kernels for 0%

commit v1 on v0

--- a/solution.py
+++ b/solution.py
@@ -5,6 +5,11 @@
 
 WINDOW = 1024
 query_scale = 168.0 ** (-0.5)
+
+
+def all_by_exchange(shard, mesh_axis, along):
+    sent = jnp.stack([shard] * lax.axis_size(mesh_axis))
+    return jnp.concatenate(lax.all_to_all(sent, mesh_axis, 0, 0), axis=along)
 
 
 def from_behind(block, axis, distance):
@@ -44,7 +49,7 @@
     def add_one(piece):
         return fold_rows(tokens, piece)
 
-    query_sum = add_one(lax.all_gather(w_query, "ctx", axis=0, tiled=True))
+    query_sum = add_one(all_by_exchange(w_query, "ctx", 0))
     summed_keys = add_one(lax.all_gather(key_weight, "ctx", axis=0, tiled=True))
     summed_values = add_one(lax.all_gather(value_weight, "ctx", axis=0, tiled=True))
     offset = lax.axis_index("ctx") * row_count

time: 407 us -> 432 us (1.061)
  the two profiles are of different devices: /device:TPU:2 before, /device:TPU:8 now
where the time goes in v1:
time: 432 us; the launch traced here: 431 us
  waiting for transfers between devices  324 us (75%)
  starting transfers between devices  52.8 us (12%)
  local copies, waits for them, and re-layouts  19.1 us (4%)
  matrix products  15.9 us (4%)
  between operations  13.7 us (3%)
  other arithmetic  5.09 us (1%)
    all_gather x1, waiting for transfers between devices, on_device(): summed_keys = add_one(lax.all_gather(key_weight, 'ctx', axis=0, tiled=True))  189 us
    all_gather x1, waiting for transfers between devices, on_device(): lax.all_gather(value_weight, 'ctx', axis=0, tiled=True)  104 us
    ppermute x6, starting transfers between devices, from_behind(): return lax.ppermute(block, axis, route)  31.9 us
    ppermute x6, waiting for transfers between devices, from_behind(): return lax.ppermute(block, axis, route)  29.9 us
    all_to_all x1, starting transfers between devices, all_by_exchange(): return jnp.concatenate(lax.all_to_all(sent, mesh_axis, 0, 0), axis=along)  20.8 us
    dot_general x3, matrix products, fold_rows(): return jnp.dot(tokens, piece, preferred_element_type=jnp.float32)  13.4 us
  transfers between devices with their start and end apart: 9, of which 5 were waited for; matrix products, arithmetic and copies ran while one was open for 6% of the time, Pallas kernels for 0%

profile of v1, /device:TPU:8, one launch (start us, length us, event | category | flops | bytes accessed | tf_op | source)
XLA Modules:
  0.0 431.0 jit_solution(4358996780785740960)
XLA Ops:
  6.5 2.6 stack.2
  9.2 20.8 %all-to-all-start = ((bf16[32,168,256]{2,1,0:T(8,128)(2,1)}), bf16[32,168,256]{2,1,0:T(8,128)(2,1)S(1)}, u32[]{:S(2)}, u32[]{:S(2)}) async-start(bf16[32,168,256]{2,1,0:T(8,128)(2,1)} %stack.2), calls=%async_computation | async-start | bytes 5505024 | tf_op jit(solution)/shard_map/all_to_all | solution.py:12
  31.5 188.9 %all-gather.5.cloned.1.call-done = bf16[5376,128]{1,0:T(8,128)(2,1)} async-done(((bf16[168,128]{1,0:T(8,128)(2,1)}), bf16[5376,128]{1,0:T(8,128)(2,1)}) %all-gather.5.cloned.1.call-update) | async-done | bytes 1376272 | tf_op jit(solution)/shard_map/all_gather | solution.py:53
  220.4 4.3 multiply_reduce_fusion.1
  224.9 1.1 fusion.19
  226.1 1.9 collective-permute-start.3
  228.0 104.3 %all-gather.3.cloned.1.call-done = bf16[5376,128]{1,0:T(8,128)(2,1)} async-done(((bf16[168,128]{1,0:T(8,128)(2,1)}), bf16[5376,128]{1,0:T(8,128)(2,1)}) %all-gather.3.cloned.1.call-update) | async-done | bytes 1376272 | tf_op jit(solution)/shard_map/all_gather | solution.py:54
  332.3 4.2 fusion.11
  336.5 1.9 collective-permute-start
  338.5 12.7 %collective-permute-start.4 = (bf16[448,1,128]{2,0,1:T(8,128)(2,1)S(1)}, bf16[448,1,128]{2,0,1:T(8,128)(2,1)S(1)}, u32[]{:S(2)}, u32[]{:S(2)}) collective-permute-start(bf16[448,1,128]{2,0,1:T(8,128)(2,1)S(1)} %collective-permute-done.3), channel_id=1, source_target_pairs={{0,16},{16,32},{32,48},{48,64},{64,80},{80,96},{96,112},{112,128},... | collective-permute-start | bytes 344072 | tf_op jit(solution)/shard_map/ppermute | solution.py:18
  351.2 17.4 %collective-permute-done = bf16[448,1,128]{2,0,1:T(8,128)(2,1)S(1)} collective-permute-done((bf16[448,1,128]{2,0,1:T(8,128)(2,1)S(1)}, bf16[448,1,128]{2,0,1:T(8,128)(2,1)S(1)}, u32[]{:S(2)}, u32[]{:S(2)}) %collective-permute-start) | collective-permute-done | bytes 114720 | tf_op jit(solution)/shard_map/ppermute | solution.py:18
  368.6 1.9 collective-permute-start.1
  370.5 1.5 and_and_fusion
  372.1 11.6 %collective-permute-start.5 = (bf16[127,1,128]{2,0,1:T(8,128)(2,1)S(1)}, bf16[127,1,128]{2,0,1:T(8,128)(2,1)}, u32[]{:S(2)}, u32[]{:S(2)}) collective-permute-start(bf16[127,1,128]{2,0,1:T(8,128)(2,1)S(1)} %slice.27), channel_id=1, source_target_pairs={{0,16},{16,32},{32,48},{48,64},{64,80},{80,96},{96,112},{112,128},... | collective-permute-start | bytes 97544 | tf_op jit(solution)/shard_map/ppermute | solution.py:18
  383.7 3.3 collective-permute-done.1
  387.7 1.9 collective-permute-start.2
  390.5 5.9 %concatenate.26 = bf16[1471,1,128]{2,0,1:T(8,128)(2,1)} concatenate(bf16[127,1,128]{2,0,1:T(8,128)(2,1)} %collective-permute-done.5, bf16[448,1,128]{2,0,1:T(8,128)(2,1)S(1)} %collective-permute-done.4, bf16[448,1,128]{2,0,1:T(8,128)(2,1)} %copy-done.4, bf16[448,1,128]{2,0,1:T(8,128)(2,1)S(1)} %pad_maximum_fusion), dimensions={0} | concatenate | bytes 753152 | tf_op jit(solution)/shard_map/concatenate | solution.py:77
  396.4 9.1 %collective-permute-done.2 = bf16[127,1,128]{2,0,1:T(8,128)(2,1)} collective-permute-done((bf16[127,1,128]{2,0,1:T(8,128)(2,1)}, bf16[127,1,128]{2,0,1:T(8,128)(2,1)}, u32[]{:S(2)}, u32[]{:S(2)}) %collective-permute-start.2) | collective-permute-done | bytes 32544 | tf_op jit(solution)/shard_map/ppermute | solution.py:18
  405.5 6.0 %concatenate.24 = bf16[1471,1,128]{2,0,1:T(8,128)(2,1)} concatenate(bf16[127,1,128]{2,0,1:T(8,128)(2,1)} %collective-permute-done.2, bf16[448,1,128]{2,0,1:T(8,128)(2,1)S(1)} %collective-permute-done.1, bf16[448,1,128]{2,0,1:T(8,128)(2,1)} %copy-done.5, bf16[448,1,128]{2,0,1:T(8,128)(2,1)} %copy-done.3), dimensions={0} | concatenate | bytes 753152 | tf_op jit(solution)/shard_map/concatenate | solution.py:78
  411.5 3.0 copy.8
  414.4 4.9 %multiply_reduce_fusion = (f32[448,2]{0,1:T(2,128)S(1)}, f32[448,2,128]{2,0,1:T(8,128)S(1)}) fusion(bf16[2,128,5376]{2,1,0:T(8,128)(2,1)} %bitcast.50, bf16[448,5376]{1,0:T(8,128)(2,1)} %param.6), kind=kOutput, calls=%fused_computation.16 | convolution fusion | flops 1233353856 | bytes 8031744 | tf_op jit(solution)/shard_map/dot_general | solution.py:40
  419.8 1.5 fusion.28
  421.3 0.9 fusion
  422.3 1.0 fusion.8
  (48 shorter events, 4.7 us)
Async XLA Ops:
  9.2 402.3 %all-to-all-start = ((bf16[32,168,256]{2,1,0:T(8,128)(2,1)}), bf16[32,168,256]{2,1,0:T(8,128)(2,1)S(1)}, u32[]{:S(2)}, u32[]{:S(2)}) async-start(bf16[32,168,256]{2,1,0:T(8,128)(2,1)} %stack.2), calls=%async_computation | async-start | bytes 5505024 | tf_op jit(solution)/shard_map/all_to_all | solution.py:12
  30.0 194.8 %copy-start.11 = (f32[128]{0:T(128)S(1)}, f32[128]{0:T(128)}, u32[]{:S(2)}) copy-start(f32[128]{0:T(128)} %param.11) | copy-start | bytes 1540
  30.0 190.5 %all-gather.5.cloned.1.call-start = ((), (), s32[]{:S(2)}) async-start(), calls=%async_computation.2 | async-start | bytes 1419264 | tf_op jit(solution)/shard_map/all_gather | solution.py:53
  30.7 301.6 %all-gather.3.cloned.1.call-start = ((), (), s32[]{:S(2)}) async-start(), calls=%async_computation.1 | async-start | bytes 1419264 | tf_op jit(solution)/shard_map/all_gather | solution.py:54
  31.5 194.5 %copy-start.8 = (f32[64]{0:T(128)}, f32[64]{0:T(128)S(1)}, u32[]{:S(2)}) copy-start(f32[64]{0:T(128)S(1)} %negate_power_fusion) | copy-start | bytes 772
  31.5 194.5 %copy-start.6 = (f32[448]{0:T(512)}, f32[448]{0:T(512)S(1)}, u32[]{:S(2)}) copy-start(f32[448]{0:T(512)S(1)} %fusion.25) | copy-start | bytes 5380
  226.1 112.4 %collective-permute-start.3 = (bf16[448,1,128]{2,0,1:T(8,128)(2,1)S(1)}, bf16[448,1,128]{2,0,1:T(8,128)(2,1)S(1)}, u32[]{:S(2)}, u32[]{:S(2)}) collective-permute-start(bf16[448,1,128]{2,0,1:T(8,128)(2,1)S(1)} %pad_maximum_fusion), channel_id=1, source_target_pairs={{0,16},{16,32},{32,48},{48,64},{64,80},{80,96},{96,112},{112,128},... | collective-permute-start | bytes 344072 | tf_op jit(solution)/shard_map/ppermute | solution.py:18
  332.3 57.3 %copy-start.7 = (f32[448]{0:T(512)S(1)}, f32[448]{0:T(512)}, u32[]{:S(2)}) copy-start(f32[448]{0:T(512)} %copy-done.6) | copy-start | bytes 5380
  332.3 57.3 %copy-start.9 = (f32[64]{0:T(128)S(1)}, f32[64]{0:T(128)}, u32[]{:S(2)}) copy-start(f32[64]{0:T(128)} %copy-done.8) | copy-start | bytes 772
  336.5 51.1 %copy-start.3 = (bf16[448,1,128]{2,0,1:T(8,128)(2,1)}, bf16[448,1,128]{2,0,1:T(8,128)(2,1)S(1)}, u32[]{:S(2)}) copy-start(bf16[448,1,128]{2,0,1:T(8,128)(2,1)S(1)} %fusion.11) | copy-start | bytes 344068
  336.5 32.1 %collective-permute-start = (bf16[448,1,128]{2,0,1:T(8,128)(2,1)S(1)}, bf16[448,1,128]{2,0,1:T(8,128)(2,1)S(1)}, u32[]{:S(2)}, u32[]{:S(2)}) collective-permute-start(bf16[448,1,128]{2,0,1:T(8,128)(2,1)S(1)} %fusion.11), channel_id=1, source_target_pairs={{0,16},{16,32},{32,48},{48,64},{64,80},{80,96},{96,112},{112,128},... | collective-permute-start | bytes 344072 | tf_op jit(solution)/shard_map/ppermute | solution.py:18
  338.5 49.2 %copy-start.4 = (bf16[448,1,128]{2,0,1:T(8,128)(2,1)}, bf16[448,1,128]{2,0,1:T(8,128)(2,1)S(1)}, u32[]{:S(2)}) copy-start(bf16[448,1,128]{2,0,1:T(8,128)(2,1)S(1)} %collective-permute-done.3) | copy-start | bytes 344068
  338.5 33.6 %collective-permute-start.4 = (bf16[448,1,128]{2,0,1:T(8,128)(2,1)S(1)}, bf16[448,1,128]{2,0,1:T(8,128)(2,1)S(1)}, u32[]{:S(2)}, u32[]{:S(2)}) collective-permute-start(bf16[448,1,128]{2,0,1:T(8,128)(2,1)S(1)} %collective-permute-done.3), channel_id=1, source_target_pairs={{0,16},{16,32},{32,48},{48,64},{64,80},{80,96},{96,112},{112,128},... | collective-permute-start | bytes 344072 | tf_op jit(solution)/shard_map/ppermute | solution.py:18
  368.6 19.1 %copy-start.5 = (bf16[448,1,128]{2,0,1:T(8,128)(2,1)}, bf16[448,1,128]{2,0,1:T(8,128)(2,1)S(1)}, u32[]{:S(2)}) copy-start(bf16[448,1,128]{2,0,1:T(8,128)(2,1)S(1)} %collective-permute-done) | copy-start | bytes 344068
  368.6 18.4 %collective-permute-start.1 = (bf16[448,1,128]{2,0,1:T(8,128)(2,1)S(1)}, bf16[448,1,128]{2,0,1:T(8,128)(2,1)S(1)}, u32[]{:S(2)}, u32[]{:S(2)}) collective-permute-start(bf16[448,1,128]{2,0,1:T(8,128)(2,1)S(1)} %collective-permute-done), channel_id=1, source_target_pairs={{0,16},{16,32},{32,48},{48,64},{64,80},{80,96},{96,112},{112,128},... | collective-permute-start | bytes 344072 | tf_op jit(solution)/shard_map/ppermute | solution.py:18
  372.1 18.4 %collective-permute-start.5 = (bf16[127,1,128]{2,0,1:T(8,128)(2,1)S(1)}, bf16[127,1,128]{2,0,1:T(8,128)(2,1)}, u32[]{:S(2)}, u32[]{:S(2)}) collective-permute-start(bf16[127,1,128]{2,0,1:T(8,128)(2,1)S(1)} %slice.27), channel_id=1, source_target_pairs={{0,16},{16,32},{32,48},{48,64},{64,80},{80,96},{96,112},{112,128},... | collective-permute-start | bytes 97544 | tf_op jit(solution)/shard_map/ppermute | solution.py:18
  387.7 17.8 %collective-permute-start.2 = (bf16[127,1,128]{2,0,1:T(8,128)(2,1)}, bf16[127,1,128]{2,0,1:T(8,128)(2,1)}, u32[]{:S(2)}, u32[]{:S(2)}) collective-permute-start(bf16[127,1,128]{2,0,1:T(8,128)(2,1)} %slice.24), channel_id=1, source_target_pairs={{0,16},{16,32},{32,48},{48,64},{64,80},{80,96},{96,112},{112,128},... | collective-permute-start | bytes 97544 | tf_op jit(solution)/shard_map/ppermute | solution.py:18
  414.4 5.0 %copy-start.10 = (f32[128]{0:T(128)S(1)}, f32[128]{0:T(128)}, u32[]{:S(2)}) copy-start(f32[128]{0:T(128)} %param.10) | copy-start | bytes 1540
  414.4 5.4 %copy-start = (pred[448,1471]{1,0:T(8,128)(4,1)S(1)}, pred[448,1471]{1,0:T(8,128)(4,1)}, u32[]{:S(2)}) copy-start(pred[448,1471]{1,0:T(8,128)(4,1)} %and_and_fusion) | copy-start | bytes 1977028
  414.4 5.4 %copy-start.1 = (bf16[1471,1,128]{2,0,1:T(8,128)(2,1)S(1)}, bf16[1471,1,128]{2,0,1:T(8,128)(2,1)}, u32[]{:S(2)}) copy-start(bf16[1471,1,128]{2,0,1:T(8,128)(2,1)} %concatenate.26) | copy-start | bytes 1129732
  419.8 2.4 copy-start.2
Sparse Core Ops, SparseCore 0:
  35.2 185.1 all-gather.4
  224.8 107.4 all-gather.2
